TPU v7x, 256 devices: a whole 4x4x8 slice. The times are simulated.
256 devices in a mesh: fsdp: 32 (over z_lo, x, core), seq: 8 (over y, z_hi).
Axes of the slice: x: 4, y: 4, z: 8 (z_hi: 2, z_lo: 4; z = z_hi * 4 + z_lo), core: 2. Of those that a mesh axis runs over, the one named last changes fastest.
Arguments:
- queries: bfloat16 [32768, 3072], P(('fsdp', 'seq')), may hold values from -1000 to 1000
- keys: bfloat16 [32768, 3072], P(('fsdp', 'seq')), may hold values from -1000 to 1000
- values: bfloat16 [32768, 3072], P(('fsdp', 'seq')), may hold values from -6 to 6
- image_ids: int32 [32, 1024], P('fsdp'), may hold values from 0 to 15, never falling along the last dimension, each value on 1 to 512 neighbouring positions
- q_gain: float32 [128], replicated, may hold values from 0.6 to 6
- k_gain: float32 [128], replicated, may hold values from 0.6 to 6
- w_out: bfloat16 [3072, 6144], P('fsdp', 'seq'), may hold values from -0.109375 to 0.109375
- grad_y: bfloat16 [32768, 6144], P('fsdp', 'seq'), may hold values from -6 to 6
Outputs:
- grad_queries: bfloat16 [32768, 24, 128], P('fsdp', 'seq')
- grad_keys: bfloat16 [32768, 24, 128], P('fsdp', 'seq')
- grad_values: bfloat16 [32768, 24, 128], P('fsdp', 'seq')
- grad_w: float32 [3072, 6144], P('fsdp', 'seq')
All inputs are finite; a program needn't handle non-finite values.
Results may differ from a plain program's by a relative error of at most 0.02.
The roundings to bfloat16 on the way count: a program that leaves them out, or rounds other values in their place, can miss the bound.
Values may be sent and summed in bfloat16 or wider, within the bound.
A program may use at most 128 MiB of HBM per device.

v0:
```python
import jax
import jax.numpy as jnp
from jax import lax
from jax.sharding import PartitionSpec as P


def norm_parts(source, gain):
    wide = source.astype(jnp.float32)
    centred = wide - jnp.mean(wide, axis=-1, keepdims=True)
    scale_inv = lax.rsqrt(jnp.mean(centred * centred, axis=-1, keepdims=True) + 1e-06)
    x_hat = centred * scale_inv
    return (x_hat, scale_inv, (x_hat * gain).astype(jnp.bfloat16))


def norm_back(grad_n, x_hat, scale_inv, gain):
    scaled = grad_n * gain
    return scale_inv * (
        scaled
        - jnp.mean(scaled, axis=-1, keepdims=True)
        - x_hat * jnp.mean(scaled * x_hat, axis=-1, keepdims=True)
    )


def probabilities(normalized_queries, normalized_keys, same_image, scale_factor):
    scores = (
        jnp.einsum(
            "krt,irt->rki", normalized_queries, normalized_keys, preferred_element_type=jnp.float32
        )
        * scale_factor
    )
    scores = jnp.where(same_image[None], scores, -1e30)
    row_top = jnp.max(scores, axis=-1, keepdims=True)
    exp_terms = jnp.exp(scores - row_top)
    return exp_terms / jnp.sum(exp_terms, axis=-1, keepdims=True)


def local(queries, keys, values, image_ids, q_gain, k_gain, w_out, grad_y):
    head_dim = q_gain.shape[0]
    tok_rows = queries.shape[0]
    heads_all = queries.shape[1] // head_dim
    scale_factor = head_dim ** (-0.5)
    q_patch = queries.reshape(tok_rows, heads_all, head_dim)
    k_patch = keys.reshape(tok_rows, heads_all, head_dim)
    v_patch = values.reshape(tok_rows, heads_all, head_dim)
    q_local, k_local, value_shard = (
        lax.all_to_all(q_patch, "seq", split_axis=1, concat_axis=0, tiled=True),
        lax.all_to_all(k_patch, "seq", split_axis=1, concat_axis=0, tiled=True),
        lax.all_to_all(v_patch, "seq", split_axis=1, concat_axis=0, tiled=True),
    )
    seq_length = q_local.shape[0]
    local_heads = q_local.shape[1]
    image_row = image_ids[0]
    same_image = image_row[:, None] == image_row[None, :]
    q_hat, q_inv, normalized_queries = norm_parts(q_local, q_gain)
    k_hat, k_inv, normalized_keys = norm_parts(k_local, k_gain)
    prob_rows = probabilities(normalized_queries, normalized_keys, same_image, scale_factor)
    probs_reduced_precision = prob_rows.astype(jnp.bfloat16)
    attended = jnp.einsum(
        "tgi,itp->gtp", probs_reduced_precision, value_shard, preferred_element_type=jnp.float32
    ).astype(jnp.bfloat16)
    attended_flat = attended.reshape(seq_length, local_heads * head_dim)
    partial_g = jnp.einsum(
        "ld,cd->lc",
        grad_y,
        lax.all_gather(w_out, "fsdp", axis=0, tiled=True),
        preferred_element_type=jnp.float32,
    )
    grad_sum = lax.psum_scatter(
        partial_g.astype(jnp.bfloat16), "seq", scatter_dimension=1, tiled=True
    )
    attention_gradient = grad_sum.reshape(seq_length, local_heads, head_dim)
    grad_values = jnp.einsum(
        "jpw,pjy->wjy",
        probs_reduced_precision,
        attention_gradient,
        preferred_element_type=jnp.float32,
    ).astype(jnp.bfloat16)
    probability_gradient = jnp.einsum(
        "krt,irt->rki", attention_gradient, value_shard, preferred_element_type=jnp.float32
    )
    row_delta = jnp.sum(prob_rows * probability_gradient, axis=-1, keepdims=True)
    score_gradient = (prob_rows * (probability_gradient - row_delta) * scale_factor).astype(
        jnp.bfloat16
    )
    normed_query_gradient = jnp.einsum(
        "tgi,itp->gtp", score_gradient, normalized_keys, preferred_element_type=jnp.float32
    )
    normed_key_gradient = jnp.einsum(
        "jpw,pjy->wjy", score_gradient, normalized_queries, preferred_element_type=jnp.float32
    )
    grad_queries = norm_back(normed_query_gradient, q_hat, q_inv, q_gain).astype(jnp.bfloat16)
    grad_keys = norm_back(normed_key_gradient, k_hat, k_inv, k_gain).astype(jnp.bfloat16)
    partial_w = jnp.einsum(
        "lc,ld->cd",
        lax.all_gather(attended_flat, "seq", axis=1, tiled=True),
        grad_y,
        preferred_element_type=jnp.float32,
    )
    summed = lax.psum_scatter(partial_w, "fsdp", scatter_dimension=0, tiled=True)
    grad_w = summed * seq_length ** (-0.5)
    return (grad_queries, grad_keys, grad_values, grad_w)


def solution(mesh):
    in_specs = (
        P(("fsdp", "seq"), None),
        P(("fsdp", "seq"), None),
        P(("fsdp", "seq"), None),
        P("fsdp", None),
        P(),
        P(),
        P("fsdp", "seq"),
        P("fsdp", "seq"),
    )
    out_specs = (
        P("fsdp", "seq", None),
        P("fsdp", "seq", None),
        P("fsdp", "seq", None),
        P("fsdp", "seq"),
    )
    return jax.shard_map(local, mesh=mesh, in_specs=in_specs, out_specs=out_specs, check_vma=False)
```

profile of v0, /device:TPU:8, one launch (start us, length us, event | category | flops | bytes accessed | tf_op | source)
XLA Modules:
  0.0 586.4 jit_solution(3500788171164991081)
XLA Ops:
  7.9 2.4 copy.60
  10.3 11.5 %all-to-all-start = ((bf16[128,24,128]{0,2,1:T(8,128)(2,1)}), bf16[128,24,128]{0,2,1:T(8,128)(2,1)S(1)}, u32[]{:S(2)}, u32[]{:S(2)}) async-start(bf16[128,24,128]{0,2,1:T(8,128)(2,1)} %bitcast), calls=%async_computation | async-start | bytes 1572864 | tf_op jit(solution)/shard_map/all_to_all | solution.py:46
  23.0 23.3 %all-to-all-done = bf16[128,24,128]{0,2,1:T(8,128)(2,1)S(1)} async-done(((bf16[128,24,128]{0,2,1:T(8,128)(2,1)}), bf16[128,24,128]{0,2,1:T(8,128)(2,1)S(1)}, u32[]{:S(2)}, u32[]{:S(2)}) %all-to-all-start) | async-done | bytes 786464 | tf_op jit(solution)/shard_map/all_to_all | solution.py:46
  46.3 6.4 %all-to-all-start.1 = ((bf16[128,24,128]{0,2,1:T(8,128)(2,1)}), bf16[128,24,128]{0,2,1:T(8,128)(2,1)S(1)}, u32[]{:S(2)}, u32[]{:S(2)}) async-start(bf16[128,24,128]{0,2,1:T(8,128)(2,1)} %bitcast.107), calls=%async_computation.1 | async-start | bytes 1572864 | tf_op jit(solution)/shard_map/all_to_all | solution.py:47
  52.7 2.3 copy.69
  55.0 11.3 %all-to-all-done.1 = bf16[128,24,128]{0,2,1:T(8,128)(2,1)S(1)} async-done(((bf16[128,24,128]{0,2,1:T(8,128)(2,1)}), bf16[128,24,128]{0,2,1:T(8,128)(2,1)S(1)}, u32[]{:S(2)}, u32[]{:S(2)}) %all-to-all-start.1) | async-done | bytes 786464 | tf_op jit(solution)/shard_map/all_to_all | solution.py:47
  66.3 7.3 %all-to-all-start.2 = ((bf16[128,24,128]{0,2,1:T(8,128)(2,1)}), bf16[128,24,128]{0,2,1:T(8,128)(2,1)}, u32[]{:S(2)}, u32[]{:S(2)}) async-start(bf16[128,24,128]{0,2,1:T(8,128)(2,1)} %bitcast.106), calls=%async_computation.2 | async-start | bytes 1572864 | tf_op jit(solution)/shard_map/all_to_all | solution.py:48
  80.4 9.0 %all-to-all-done.2 = bf16[128,24,128]{0,2,1:T(8,128)(2,1)} async-done(((bf16[128,24,128]{0,2,1:T(8,128)(2,1)}), bf16[128,24,128]{0,2,1:T(8,128)(2,1)}, u32[]{:S(2)}, u32[]{:S(2)}) %all-to-all-start.2) | async-done | bytes 786464 | tf_op jit(solution)/shard_map/all_to_all | solution.py:48
  89.4 2.3 copy.71
  93.3 2.3 copy-done.3
  99.2 11.0 %fusion.54 = (f32[3,1024]{1,0:T(4,128)S(1)}, f32[3,1024,1024]{1,2,0:T(8,128)}) fusion(pred[1024,1024]{0,1:T(8,128)(4,1)S(1)} %copy-done.12, bf16[1024,3,128]{0,2,1:T(8,128)(2,1)} %get-tuple-element.32, bf16[1024,3,128]{0,2,1:T(8,128)(2,1)} %get-tuple-element.33), kind=kOutput, calls=%fused_computation.65 | convolution fusion | flops 817890304 | bytes 15216640 | tf_op jit(solution)/shard_map/sub | solution.py:33
  110.2 6.6 %fusion.38 = bf16[3,1024,128]{1,2,0:T(8,128)(2,1)} fusion(bf16[1024,3,128]{2,0,1:T(8,128)(2,1)S(1)} %bitcast.104, f32[3,1024,1024]{1,2,0:T(8,128)} %get-tuple-element.29, f32[3,1024]{1,0:T(4,128)S(1)} %get-tuple-element.28), kind=kOutput, calls=%fused_computation.45 | convolution fusion | flops 811991040 | bytes 14168064 | tf_op jit(solution)/shard_map/tgi,itp->gtp/dot_general | solution.py:58
  117.1 9.4 %convolution_convert_fusion = bf16[1024,3072]{1,0:T(8,128)(2,1)} fusion(bf16[1024,768]{1,0:T(8,128)(2,1)S(1)} %copy-done, bf16[3072,768]{1,0:T(8,128)(2,1)} %all-gather.3.cloned.1.call-done), kind=kOutput, calls=%fused_computation.14 | convolution fusion | flops 4834983936 | bytes 12582912 | tf_op jit(solution)/shard_map/ld,cd->lc/dot_general | solution.py:62
  126.5 8.7 %copy.92 = bf16[1024,3072]{0,1:T(8,128)(2,1)} copy(bf16[1024,3072]{1,0:T(8,128)(2,1)} %convolution_convert_fusion) | data formatting | bytes 12582912
  135.2 130.9 %all-gather.5.cloned.1.call-done = bf16[1024,3072]{0,1:T(8,128)(2,1)} async-done(((bf16[1024,384]{0,1:T(8,128)(2,1)}), bf16[1024,3072]{0,1:T(8,128)(2,1)}) %all-gather.5.cloned.1.call-update) | async-done | bytes 6291472 | tf_op jit(solution)/shard_map/all_gather | solution.py:95
  266.1 10.0 %fusion.59 = f32[3072,768]{1,0:T(8,128)} fusion(bf16[1024,3072]{0,1:T(8,128)(2,1)} %all-gather.5.cloned.1.call-done, bf16[1024,768]{1,0:T(8,128)(2,1)S(1)} %copy-done), kind=kOutput, calls=%fused_computation.66 | convolution fusion | flops 4831838208 | bytes 17301504 | tf_op jit(solution)/shard_map/lc,ld->cd/dot_general | solution.py:93
  276.1 143.7 %reduce-scatter.7.cloned.1.call-done = bf16[384,1024]{1,0:T(8,128)(2,1)} async-done(((bf16[3072,1024]{1,0:T(8,128)(2,1)}), bf16[384,1024]{1,0:T(8,128)(2,1)}) %reduce-scatter.7.cloned.1.call-update) | async-done | bytes 786448
  419.8 7.5 %fusion.60 = f32[3,1024,1024]{1,2,0:T(8,128)} fusion(bf16[1024,3,128]{2,0,1:T(8,128)(2,1)S(1)} %bitcast.105, bf16[1024,3,128]{0,2,1:T(8,128)(2,1)} %bitcast.108), kind=kOutput, calls=%fused_computation.67 | convolution fusion | flops 805306368 | bytes 14155776 | tf_op jit(solution)/shard_map/krt,irt->rki/dot_general | solution.py:78
  427.3 19.4 %bitcast_reduce_fusion.1 = (f32[1024,3]{0,1:T(4,128)S(1)}, f32[1024,3]{0,1:T(4,128)S(1)}, f32[3,128,1024]{2,1,0:T(8,128)}) fusion(f32[1024,3]{0,1:T(4,128)S(1)} %rsqrt_bitcast_fusion.1, f32[1024,3]{0,1:T(4,128)S(1)} %get-tuple-element.25, f32[8,3,16,8,128]{4,3,2,1,0:T(8,128)S(1)} %bitcast.102, f32[128]{0:T(128)S(1)} %copy-done.18, ...), kind=kOutput, calls=%fused_computation.33 | convolution fusion | flops 829683712 | bytes 29159936 | tf_op jit(solution)/shard_map/tgi,itp->gtp/dot_general | solution.py:85
  446.7 1.8 fusion.27
  450.3 19.6 %bitcast_reduce_fusion = (f32[1024,3]{0,1:T(4,128)S(1)}, f32[1024,3]{0,1:T(4,128)S(1)}, f32[3,128,1024]{2,1,0:T(8,128)}) fusion(f32[1024,3]{0,1:T(4,128)S(1)} %rsqrt_bitcast_fusion, f32[1024,3]{0,1:T(4,128)S(1)} %get-tuple-element.26, f32[8,3,16,8,128]{4,3,2,1,0:T(8,128)S(1)} %bitcast.99, f32[128]{0:T(128)S(1)} %copy-done.19, ...), kind=kOutput, calls=%fused_computation.26 | convolution fusion | flops 829683712 | bytes 29159936 | tf_op jit(solution)/shard_map/jpw,pjy->wjy/dot_general | solution.py:88
  469.9 1.7 fusion.23
  472.8 7.0 %fusion.43 = bf16[1024,3,128]{0,2,1:T(8,128)(2,1)S(1)} fusion(bf16[1024,3,128]{0,2,1:T(8,128)(2,1)S(1)} %bitcast.109, f32[3,1024,1024]{1,2,0:T(8,128)} %get-tuple-element.29, f32[3,1024]{1,0:T(4,128)S(1)} %get-tuple-element.28), kind=kOutput, calls=%fused_computation.47 | convolution fusion | flops 811991040 | bytes 14168064 | tf_op jit(solution)/shard_map/jpw,pjy->wjy/dot_general | solution.py:72
  481.1 97.2 %reduce-scatter.5.cloned.1.call-done = f32[96,768]{1,0:T(8,128)} async-done(((f32[3072,768]{1,0:T(8,128)}), f32[96,768]{1,0:T(8,128)}) %reduce-scatter.5.cloned.1.call-update) | async-done | bytes 294928 | tf_op jit(solution)/shard_map/reduce_scatter | solution.py:99
  (71 shorter events, 19.7 us)
Async XLA Ops:
  7.2 109.9 %copy-start = (bf16[1024,768]{1,0:T(8,128)(2,1)S(1)}, bf16[1024,768]{1,0:T(8,128)(2,1)}, u32[]{:S(2)}) copy-start(bf16[1024,768]{1,0:T(8,128)(2,1)} %param.15) | copy-start | bytes 4718596
  7.2 109.9 %all-gather.3.cloned.1.call-start = ((), (), s32[]{:S(2)}) async-start(), calls=%async_computation.5 | async-start | bytes 4866048 | tf_op jit(solution)/shard_map/all_gather | solution.py:65
  7.9 13.9 %copy-start.14 = (bf16[128,3072]{1,0:T(8,128)(2,1)S(1)}, bf16[128,3072]{1,0:T(8,128)(2,1)}, u32[]{:S(2)}) copy-start(bf16[128,3072]{1,0:T(8,128)(2,1)} %param.9) | copy-start | bytes 2359300
  10.3 36.0 %all-to-all-start = ((bf16[128,24,128]{0,2,1:T(8,128)(2,1)}), bf16[128,24,128]{0,2,1:T(8,128)(2,1)S(1)}, u32[]{:S(2)}, u32[]{:S(2)}) async-start(bf16[128,24,128]{0,2,1:T(8,128)(2,1)} %bitcast), calls=%async_computation | async-start | bytes 1572864 | tf_op jit(solution)/shard_map/all_to_all | solution.py:46
  46.3 8.7 %copy-start.8 = (bf16[128,24,128]{0,2,1:T(8,128)(2,1)}, bf16[128,24,128]{0,2,1:T(8,128)(2,1)S(1)}, u32[]{:S(2)}) copy-start(bf16[128,24,128]{0,2,1:T(8,128)(2,1)S(1)} %all-to-all-done) | copy-start | bytes 2359300
  46.3 20.0 %all-to-all-start.1 = ((bf16[128,24,128]{0,2,1:T(8,128)(2,1)}), bf16[128,24,128]{0,2,1:T(8,128)(2,1)S(1)}, u32[]{:S(2)}, u32[]{:S(2)}) async-start(bf16[128,24,128]{0,2,1:T(8,128)(2,1)} %bitcast.107), calls=%async_computation.1 | async-start | bytes 1572864 | tf_op jit(solution)/shard_map/all_to_all | solution.py:47
  52.7 21.0 %copy-start.17 = (s32[1,1024]{1,0:T(1,128)S(1)}, s32[1,1024]{1,0:T(1,128)}, u32[]{:S(2)}) copy-start(s32[1,1024]{1,0:T(1,128)} %param.11) | copy-start | bytes 12292
  66.3 7.3 %copy-start.9 = (bf16[128,24,128]{0,2,1:T(8,128)(2,1)}, bf16[128,24,128]{0,2,1:T(8,128)(2,1)S(1)}, u32[]{:S(2)}) copy-start(bf16[128,24,128]{0,2,1:T(8,128)(2,1)S(1)} %all-to-all-done.1) | copy-start | bytes 2359300
  66.3 23.1 %all-to-all-start.2 = ((bf16[128,24,128]{0,2,1:T(8,128)(2,1)}), bf16[128,24,128]{0,2,1:T(8,128)(2,1)}, u32[]{:S(2)}, u32[]{:S(2)}) async-start(bf16[128,24,128]{0,2,1:T(8,128)(2,1)} %bitcast.106), calls=%async_computation.2 | async-start | bytes 1572864 | tf_op jit(solution)/shard_map/all_to_all | solution.py:48
  73.7 192.5 %all-gather.5.cloned.1.call-start = ((), (), s32[]{:S(2)}) async-start(), calls=%async_computation.6 | async-start | bytes 7077888 | tf_op jit(solution)/shard_map/all_gather | solution.py:95
  93.1 4.5 copy-start.6
  93.1 2.5 copy-start.3
  93.3 4.3 copy-start.4
  95.6 1.9 copy-start.18
  95.6 1.9 copy-start.19
  97.6 1.6 copy-start.12
  99.2 11.0 %copy-start.11 = (bf16[8,128,3,128]{3,1,0,2:T(8,128)(2,1)S(1)}, bf16[8,128,3,128]{3,1,0,2:T(8,128)(2,1)}, u32[]{:S(2)}) copy-start(bf16[8,128,3,128]{3,1,0,2:T(8,128)(2,1)} %copy.71) | copy-start | bytes 2359300
  116.8 302.9 %reduce-scatter.7.cloned.1.call-start = ((), (), s32[]{:S(2)}) async-start(), calls=%async_computation.8 | async-start | bytes 7077888
  135.2 443.0 %reduce-scatter.5.cloned.1.call-start = ((), (), s32[]{:S(2)}) async-start(), calls=%async_computation.7 | async-start | bytes 9732096 | tf_op jit(solution)/shard_map/reduce_scatter | solution.py:99
  419.8 7.6 %copy-start.7 = (f32[128,24,128]{0,2,1:T(8,128)S(1)}, f32[128,24,128]{0,2,1:T(8,128)}, u32[]{:S(2)}) copy-start(f32[128,24,128]{0,2,1:T(8,128)} %copy-done.6) | copy-start | bytes 4718596
  419.8 7.6 %copy-start.16 = (bf16[1024,3,128]{0,2,1:T(8,128)(2,1)S(1)}, bf16[1024,3,128]{0,2,1:T(8,128)(2,1)}, u32[]{:S(2)}) copy-start(bf16[1024,3,128]{0,2,1:T(8,128)(2,1)} %get-tuple-element.33) | copy-start | bytes 2359300
  446.7 3.0 copy-start.15
  448.6 1.7 copy-start.5
  472.8 107.1 %copy-start.1 = (bf16[1024,768]{1,0:T(8,128)(2,1)S(1)}, bf16[1024,768]{1,0:T(8,128)(2,1)}, u32[]{:S(2)}) copy-start(bf16[1024,768]{1,0:T(8,128)(2,1)} %param.15) | copy-start | bytes 4718596
  (3 other events, 3.7 us)
Sparse Core Ops, SparseCore 0:
  9.9 106.4 all-gather.2
  119.6 146.5 all-gather.4
  270.3 149.3 reduce-scatter.6
  422.4 155.7 reduce-scatter.4
where the time goes:
time: 587 us; the launch traced here: 586 us
  waiting for transfers between devices  416 us (71%)
  matrix products  90.5 us (15%)
  local copies, waits for them, and re-layouts  27.2 us (5%)
  starting transfers between devices  25.6 us (4%)
  between operations  14 us (2%)
  other arithmetic  13 us (2%)
    unnamed x5, waiting for transfers between devices  144 us
    all_gather x1, waiting for transfers between devices, local(): lax.all_gather(attended_flat, 'seq', axis=1, tiled=True)  131 us
    reduce_scatter x1, waiting for transfers between devices, local(): lax.psum_scatter(partial_w, 'fsdp', scatter_dimension=0, tiled=True)  97.2 us
    all_to_all x1, waiting for transfers between devices, local(): lax.all_to_all(q_patch, 'seq', split_axis=1, concat_axis=0, tiled=True)  23.3 us
    unnamed x47, local copies, waits for them, and re-layouts  22.1 us
    dot_general x1, matrix products, local(): jnp.einsum('jpw,pjy->wjy', score_gradient, normalized_queries, preferred_...  19.6 us
    dot_general x1, matrix products, local(): jnp.einsum('tgi,itp->gtp', score_gradient, normalized_keys, preferred_ele...  19.4 us
  transfers between devices with their start and end apart: 7, of which 6 were waited for; matrix products, arithmetic and copies ran while one was open for 21% of the time, Pallas kernels for 0%

commit v1 on v0

v1 whole, which is shorter than its diff:
```python
import jax
import jax.numpy as jnp
from jax import lax
from jax.experimental import pallas as pl
from jax.experimental.pallas import tpu as pltpu
from jax.sharding import PartitionSpec as P

MESH = pl.DeviceIdType.MESH
F32 = jnp.float32
BF16 = jnp.bfloat16
HD = 128
HL = 3
HW = HL * HD
SEQ = 1024
TOK = 128
COLS = 768
CH = 256
NCH = SEQ // CH
SCALE = HD ** (-0.5)
W_SCALE = SEQ ** (-0.5)
SEGMENTS = (
    ((0, 96, 0, 0), (96, 32, 1, 0)),
    ((0, 64, 1, 32), (64, 64, 0, 96)),
    ((0, 32, 0, 160), (32, 96, 1, 96)),
)
N_QKV = 21


def nt(a, b):
    return lax.dot_general(a, b, (((1,), (1,)), ((), ())), preferred_element_type=F32)


def nn(a, b):
    return lax.dot_general(a, b, (((1,), (0,)), ((), ())), preferred_element_type=F32)


def stats(source):
    wide = source.astype(F32)
    centred = wide - jnp.mean(wide, axis=-1, keepdims=True)
    inv = lax.rsqrt(jnp.mean(centred * centred, axis=-1, keepdims=True) + 1e-06)
    return centred * inv, inv


def norm_back(grad_n, source, gain):
    x_hat, inv = stats(source)
    u = grad_n * gain
    return inv * (
        u
        - jnp.mean(u, axis=-1, keepdims=True)
        - x_hat * jnp.mean(u * x_hat, axis=-1, keepdims=True)
    )


def kernel(
    q_in, k_in, v_in, ids_row, ids_col, qgain, kgain, w_in, gy,
    gq, gk, gv, gw,
    qkv, qn, kn, knt, vt, gyo, wb, prob, pg, rsr, att, ga, dk, dv,
    acc, cbuf, crecv, xrecv, zsend, zrecv, fsend, frecv,
    s_own, s_qkv, r_qkv, s_w, r_w, s_gy, r_gy, s_rs, r_rs, s_at, r_at,
    s_c, r_c, s_x, r_x, s_z, r_z, s_f, r_f,
):
    f = lax.axis_index("fsdp")
    s = lax.axis_index("seq")
    zl, x, c = f // 8, (f // 2) % 4, f % 2
    y, zh = s // 2, s % 2
    oc = 1 - c
    ozh = 1 - zh
    xf = (x + 2) % 4
    xlo, xhi = x % 2, x // 2

    def dev(zl_=None, x_=None, c_=None, y_=None, zh_=None):
        zl_ = zl if zl_ is None else zl_
        x_ = x if x_ is None else x_
        c_ = c if c_ is None else c_
        y_ = y if y_ is None else y_
        zh_ = zh if zh_ is None else zh_
        return (zl_ * 8 + x_ * 2 + c_, y_ * 2 + zh_)

    def send(src, dst, ss, rs, where):
        return pltpu.make_async_remote_copy(
            src_ref=src, dst_ref=dst, send_sem=ss, recv_sem=rs,
            device_id=where, device_id_type=MESH,
        )

    offs = [(dy, 1) for dy in range(4)] + [(dy, 0) for dy in range(1, 4)]

    def seq_partner(dy, dz, sign=1):
        yy = (y + sign * dy + 4) % 4
        zz = (zh + dz) % 2
        return yy, zz

    barrier = pltpu.get_barrier_semaphore()
    partners = [dev(y_=a, zh_=b) for a, b in (seq_partner(dy, dz) for dy, dz in offs)]
    partners += [dev(x_=(x + o) % 4) for o in (1, 2, 3)]
    partners += [dev(zl_=(zl + o) % 4) for o in (1, 2, 3)]
    partners += [dev(c_=oc), dev(x_=xf, zh_=ozh)]
    for p in partners:
        pl.semaphore_signal(barrier, inc=1, device_id=p, device_id_type=MESH)
    pl.semaphore_wait(barrier, len(partners))

    same = xhi == zh
    w_own = wb.at[xhi, zl, xlo, c]
    w_swap = send(w_in, wb.at[1 - xhi, zl, xlo, c], s_w.at[0], r_w.at[0], dev(x_=xf, zh_=ozh))
    w_copy = pltpu.make_async_copy(w_in, w_own, s_own.at[3])

    @pl.when(same)
    def _():
        w_copy.start()

    @pl.when(jnp.logical_not(same))
    def _():
        w_swap.start()

    sources = (q_in, k_in, v_in)
    qkv_copies = []
    for i, (dy, dz) in enumerate(offs):
        yy, zz = seq_partner(dy, dz)
        ps = yy * 2 + zz
        cols = pl.ds(pl.multiple_of(ps * HW, 128), HW)
        rows = pl.ds(pl.multiple_of(s * TOK, TOK), TOK)
        for a in range(3):
            n = i * 3 + a
            qkv_copies.append(
                send(sources[a].at[:, cols], qkv.at[a, rows, :], s_qkv.at[n], r_qkv.at[n],
                     dev(y_=yy, zh_=zz))
            )
    own_copies = []
    for a in range(3):
        cols = pl.ds(pl.multiple_of(s * HW, 128), HW)
        rows = pl.ds(pl.multiple_of(s * TOK, TOK), TOK)
        own_copies.append(
            pltpu.make_async_copy(sources[a].at[:, cols], qkv.at[a, rows, :], s_own.at[a])
        )
    for cp in qkv_copies[12:]:
        cp.start()
    for cp in own_copies:
        cp.start()

    @pl.when(same)
    def _():
        w_copy.wait()

    @pl.when(jnp.logical_not(same))
    def _():
        w_swap.wait()

    wz = [
        send(w_own, w_own, s_w.at[o], r_w.at[o], dev(zl_=(zl + o) % 4)) for o in (1, 2, 3)
    ]
    for cp in wz:
        cp.start()
    for cp in qkv_copies[:12]:
        cp.start()
    for cp in wz:
        cp.wait()
    w_line = wb.at[xhi, :, xlo, c]
    wx = [
        send(w_line, w_line, s_w.at[3 + o], r_w.at[3 + o], dev(x_=(x + o) % 4))
        for o in (1, 2, 3)
    ]
    for cp in wx:
        cp.start()
    for cp in wx:
        cp.wait()
    wc = []
    for i in range(2):
        half = wb.at[i, :, :, c]
        wc.append(send(half, half, s_w.at[7 + i], r_w.at[7 + i], dev(c_=oc)))
    for cp in wc:
        cp.start()

    gy_copies = []
    for t in range(NCH):
        rows = pl.ds(t * CH, CH)
        gy_copies.append(
            send(gy.at[rows, :], gyo.at[rows, :], s_gy.at[t], r_gy.at[t], dev(zh_=ozh))
        )

    for cp in own_copies:
        cp.wait()
    for cp in qkv_copies:
        cp.wait_send()
    gy_copies[0].start()
    gy_copies[1].start()
    for cp in qkv_copies:
        cp.wait_recv()

    gain_q = qgain[...]
    gain_k = kgain[...]
    for h in range(HL):
        hc = pl.ds(h * HD, HD)

        def norm_step(t, carry, h=h, hc=hc):
            rows = pl.ds(pl.multiple_of(t * CH, CH), CH)
            qh, _ = stats(qkv[0, rows, hc])
            qn[rows, hc] = (qh * gain_q).astype(BF16)
            kh, _ = stats(qkv[1, rows, hc])
            knv = kh * gain_k
            kn[rows, hc] = knv.astype(BF16)
            knt[hc, rows] = knv.T.astype(BF16)
            vt[hc, rows] = qkv[2, rows, hc].astype(F32).T.astype(BF16)
            return carry

        lax.fori_loop(0, NCH, norm_step, 0)

    for h in range(HL):
        hc = pl.ds(h * HD, HD)

        def fwd_step(t, carry, h=h, hc=hc):
            rows = pl.ds(pl.multiple_of(t * CH, CH), CH)
            st = nt(kn[:, hc], qn[rows, hc]) * SCALE
            keep = ids_col[:, 0:1] == ids_row[:, rows]
            st = jnp.where(keep, st, -1e30)
            top = jnp.max(st, axis=0, keepdims=True)
            e = jnp.exp(st - top)
            total = jnp.sum(e, axis=0, keepdims=True)
            pt = e * (1.0 / total)
            prob[h, :, rows] = pt
            at = nn(vt[hc, :], pt.astype(BF16)).astype(BF16)
            for first, count, half, place in SEGMENTS[h]:
                at_rows = pl.ds(pl.multiple_of(y * 192 + place, 16), count)
                att[half, at_rows, rows] = at[first : first + count, :]
            return carry

        lax.fori_loop(0, NCH, fwd_step, 0)

    my_att = att.at[:, pl.ds(pl.multiple_of(y * 192, 16), 192), :]
    at_copies = [
        send(my_att, my_att, s_at.at[o - 1], r_at.at[o - 1], dev(y_=(y + o) % 4))
        for o in (1, 2, 3)
    ]
    for cp in at_copies:
        cp.start()
    for cp in wc:
        cp.wait()

    rs_copies = {}

    def grad_chunk(t):
        rows = pl.ds(t * CH, CH)
        gy_copies[t].wait()
        if t + 2 < NCH:
            gy_copies[t + 2].start()
        for o in (1, 2, 3, 0):
            yy = (y + o) % 4
            blk_own = wb[zh, yy].reshape(HW, COLS)
            blk_other = wb[ozh, yy].reshape(HW, COLS)
            val = nt(gy[rows, :], blk_own) + nt(gyo[rows, :], blk_other)
            pg[yy, rows, :] = val.astype(BF16)
            if o:
                cp = send(pg.at[yy, rows, :], rsr.at[o - 1, rows, :],
                          s_rs.at[t * 3 + o - 1], r_rs.at[t * 3 + o - 1], dev(y_=yy))
                rs_copies[(t, o)] = cp
                cp.start()

    def backward_chunk(t):
        rows = pl.ds(t * CH, CH)
        for o in (1, 2, 3):
            rs_copies[(t, o)].wait()
        total = pg[y, rows, :].astype(F32)
        for o in range(3):
            total = total + rsr[o, rows, :].astype(F32)
        ga[...] = total.astype(BF16)

        def head(h, carry):
            hc = pl.ds(pl.multiple_of(h * HD, HD), HD)
            do = ga[:, hc]
            dpt = nt(qkv[2, :, hc], do)
            pt = prob[h, :, rows]
            delta = jnp.sum(pt * dpt, axis=0, keepdims=True)
            dst = (pt * (dpt - delta) * SCALE).astype(BF16)
            dv_new = nn(pt.astype(BF16), do)
            dk_new = nn(dst, qn[rows, hc])
            if t == 0:
                dv[:, hc] = dv_new
                dk[:, hc] = dk_new
            else:
                dv[:, hc] += dv_new
                dk[:, hc] += dk_new
            dqt = nn(knt[hc, :], dst)
            gq[rows, hc] = norm_back(dqt.T, qkv[0, rows, hc], gain_q).astype(BF16)
            return carry

        lax.fori_loop(0, HL, head, 0)

    def weight_products(p):
        right = gy if p == 0 else gyo
        for half, mine in ((oc, False), (c, True)):
            def step(i, carry, half=half, mine=mine):
                a_rows = pl.ds(pl.multiple_of(i * 192, 64), 192)
                val = nn(att[half, a_rows, :], right[...]).reshape(4, 48, COLS)
                if mine:
                    acc[p, i] = val
                else:
                    cbuf[p, i] = val.astype(BF16)
                return carry

            lax.fori_loop(0, 4, step, 0)
            if not mine:
                core_copies[p].start()

    core_copies = [
        send(cbuf.at[p], crecv.at[p], s_c.at[p], r_c.at[p], dev(c_=oc)) for p in range(2)
    ]

    x_copies = {}

    def to_x(p):
        core_copies[p].wait()

        def step(i, carry):
            val = acc[p, i] + crecv[p, i].astype(F32)
            acc[p, i] = val
            cbuf[p, i] = val.astype(BF16)
            return carry

        lax.fori_loop(0, 4, step, 0)
        for o in (1, 2, 3):
            xx = (x + o) % 4
            quarter = (xx % 2) * 2 + xx // 2
            n = p * 3 + o - 1
            cp = send(cbuf.at[p, :, quarter], xrecv.at[p, o - 1], s_x.at[n], r_x.at[n],
                      dev(x_=xx))
            x_copies[(p, o)] = cp
            cp.start()

    z_copies = {}

    def to_z(p):
        for o in (1, 2, 3):
            x_copies[(p, o)].wait()
        quarter = xlo * 2 + xhi

        def step(i, carry):
            val = acc[p, i, quarter]
            for o in range(3):
                val = val + xrecv[p, o, i].astype(F32)
            acc[p, i, quarter] = val
            zsend[p, i] = val.astype(BF16)
            return carry

        lax.fori_loop(0, 4, step, 0)
        for o in (1, 2, 3):
            zz = (zl + o) % 4
            n = p * 3 + o - 1
            cp = send(zsend.at[p, zz], zrecv.at[p, o - 1], s_z.at[n], r_z.at[n], dev(zl_=zz))
            z_copies[(p, o)] = cp
            cp.start()

    def reduced(p):
        for o in (1, 2, 3):
            z_copies[(p, o)].wait()
        val = acc[p, zl, xlo * 2 + xhi]
        for o in range(3):
            val = val + zrecv[p, o].astype(F32)
        return val * W_SCALE

    mine_rows = pl.ds(pl.multiple_of(xhi * 48, 16), 48)
    other_rows = pl.ds(pl.multiple_of((1 - xhi) * 48, 16), 48)
    f_x = send(fsend.at[0], frecv.at[0], s_f.at[0], r_f.at[0], dev(x_=xf))
    f_z = send(fsend.at[1], frecv.at[1], s_f.at[1], r_f.at[1], dev(zh_=ozh))
    f_xz = send(fsend.at[1], frecv.at[2], s_f.at[2], r_f.at[2], dev(x_=xf, zh_=ozh))

    def finish_own():
        val = reduced(0)

        @pl.when(same)
        def _():
            gw[mine_rows, :] = val

        @pl.when(jnp.logical_not(same))
        def _():
            fsend[0] = val.astype(BF16)
            f_x.start()

    def finish_other():
        fsend[1] = reduced(1).astype(BF16)

        @pl.when(same)
        def _():
            f_z.start()
            f_x.wait_recv()
            gw[other_rows, :] = frecv[0].astype(F32)
            f_z.wait_send()

        @pl.when(jnp.logical_not(same))
        def _():
            f_xz.start()
            f_x.wait_send()
            f_z.wait_recv()
            gw[mine_rows, :] = frecv[1].astype(F32)
            f_xz.wait()
            gw[other_rows, :] = frecv[2].astype(F32)

    grad_chunk(0)
    grad_chunk(1)
    for cp in at_copies:
        cp.wait()
    weight_products(0)
    backward_chunk(0)
    to_x(0)
    grad_chunk(2)
    backward_chunk(1)
    to_z(0)
    grad_chunk(3)
    weight_products(1)
    to_x(1)
    finish_own()
    backward_chunk(2)
    to_z(1)
    backward_chunk(3)
    for h in range(HL):
        hc = pl.ds(h * HD, HD)

        def key_step(t, carry, hc=hc):
            rows = pl.ds(pl.multiple_of(t * CH, CH), CH)
            gk[rows, hc] = norm_back(dk[rows, hc], qkv[1, rows, hc], gain_k).astype(BF16)
            gv[rows, hc] = dv[rows, hc].astype(BF16)
            return carry

        lax.fori_loop(0, NCH, key_step, 0)
    finish_other()


def local(queries, keys, values, image_ids, q_gain, k_gain, w_out, grad_y):
    ids_col = jnp.broadcast_to(image_ids.reshape(SEQ, 1), (SEQ, 128))
    vm = pl.BlockSpec(memory_space=pltpu.VMEM)
    hb = pl.BlockSpec(memory_space=pl.ANY)
    dma = lambda n: pltpu.SemaphoreType.DMA((n,))
    vmem = pltpu.VMEM
    scratch = [
        vmem((3, SEQ, HW), BF16),
        vmem((SEQ, HW), BF16),
        vmem((SEQ, HW), BF16),
        vmem((HW, SEQ), BF16),
        vmem((HW, SEQ), BF16),
        vmem((SEQ, COLS), BF16),
        vmem((2, 4, 2, 2, 96, COLS), BF16),
        vmem((HL, SEQ, SEQ), F32),
        vmem((4, SEQ, HW), BF16),
        vmem((3, SEQ, HW), BF16),
        vmem((2, 768, SEQ), BF16),
        vmem((CH, HW), BF16),
        vmem((SEQ, HW), F32),
        vmem((SEQ, HW), F32),
        vmem((2, 4, 4, 48, COLS), F32),
        vmem((2, 4, 4, 48, COLS), BF16),
        vmem((2, 4, 4, 48, COLS), BF16),
        vmem((2, 3, 4, 48, COLS), BF16),
        vmem((2, 4, 48, COLS), BF16),
        vmem((2, 3, 48, COLS), BF16),
        vmem((2, 48, COLS), BF16),
        vmem((3, 48, COLS), BF16),
        dma(4),
        dma(N_QKV), dma(N_QKV),
        dma(9), dma(9),
        dma(NCH), dma(NCH),
        dma(3 * NCH), dma(3 * NCH),
        dma(3), dma(3),
        dma(2), dma(2),
        dma(6), dma(6),
        dma(6), dma(6),
        dma(3), dma(3),
    ]
    gq, gk, gv, gw = pl.pallas_call(
        kernel,
        out_shape=(
            jax.ShapeDtypeStruct((SEQ, HW), BF16),
            jax.ShapeDtypeStruct((SEQ, HW), BF16),
            jax.ShapeDtypeStruct((SEQ, HW), BF16),
            jax.ShapeDtypeStruct((96, COLS), F32),
        ),
        in_specs=[hb, hb, hb, vm, vm, vm, vm, vm, vm],
        out_specs=(vm, vm, vm, vm),
        scratch_shapes=scratch,
        compiler_params=pltpu.CompilerParams(
            collective_id=0, has_side_effects=True, vmem_limit_bytes=62 * 1024 * 1024
        ),
        name="attention_backward",
    )(
        queries, keys, values, image_ids, ids_col,
        q_gain.reshape(1, HD), k_gain.reshape(1, HD), w_out, grad_y,
    )
    heads = lambda a: a.reshape(SEQ, HL, HD)
    return heads(gq), heads(gk), heads(gv), gw


def solution(mesh):
    in_specs = (
        P(("fsdp", "seq"), None),
        P(("fsdp", "seq"), None),
        P(("fsdp", "seq"), None),
        P("fsdp", None),
        P(),
        P(),
        P("fsdp", "seq"),
        P("fsdp", "seq"),
    )
    out_specs = (
        P("fsdp", "seq", None),
        P("fsdp", "seq", None),
        P("fsdp", "seq", None),
        P("fsdp", "seq"),
    )
    return jax.shard_map(local, mesh=mesh, in_specs=in_specs, out_specs=out_specs, check_vma=False)
```

time: 587 us -> 246 us (0.42)
  the two profiles are of different devices: /device:TPU:8 before, /device:TPU:36 now
where the time goes in v1:
time: 246 us
  Pallas kernels  238 us (97%)
  local copies, waits for them, and re-layouts  7.92 us (3%)
    pallas_call x1, Pallas kernels, local(): pl.pallas_call(kernel, out_shape=(jax.ShapeDtypeStruct((SEQ, HW), BF16),...  238 us

profile of v1, /device:TPU:36, one launch (start us, length us, event | category | flops | bytes accessed | tf_op | source)
XLA Modules:
  0.0 246.3 jit_solution(11596554894369541105)
XLA Ops:
  0.6 1.7 broadcast_in_dim.8.ids_col
  2.3 237.7 %attention_backward.1 = (bf16[1024,384]{1,0:T(8,128)(2,1)}, bf16[1024,384]{1,0:T(8,128)(2,1)}, bf16[1024,384]{1,0:T(8,128)(2,1)}, f32[96,768]{1,0:T(8,128)}) custom-call(bf16[128,3072]{1,0:T(8,128)(2,1)} %q_in.1, bf16[128,3072]{1,0:T(8,128)(2,1)} %k_in.1, bf16[128,3072]{1,0:T(8,128)(2,1)} %v_in.1, s32[1,1024]{1,0:T(1,128)} %ids_row.1, ...), custom_call_target="tpu_custom_call" | custom-call | tf_op jit(solution)/shard_map/attention_backward/pallas_call | solution.py:465
  240.0 0.0 copy-start.1
  240.0 1.5 copy.15
  241.5 1.2 copy.18
  242.7 0.0 copy-done.1
  242.7 0.0 copy-start
  242.7 0.3 copy.16
  243.0 1.2 copy.19
  244.1 0.0 copy-done
  244.1 0.0 copy-start.2
  244.1 0.3 copy.17
  244.4 1.2 copy.20
  245.6 0.0 copy-done.2
  245.6 0.7 copy.22
Async XLA Ops:
  240.0 2.6 %copy-start.1 = (bf16[1024,384]{1,0:T(8,128)(2,1)S(1)}, bf16[1024,384]{1,0:T(8,128)(2,1)}, u32[]{:S(2)}) copy-start(bf16[1024,384]{1,0:T(8,128)(2,1)} %get-tuple-element.9) | copy-start | bytes 2359300
  242.7 1.5 copy-start
  244.1 1.5 copy-start.2

commit v2 on v1

v2 whole, which is shorter than its diff:
```python
import jax
import jax.numpy as jnp
from jax import lax
from jax.experimental import pallas as pl
from jax.experimental.pallas import tpu as pltpu
from jax.sharding import PartitionSpec as P

MESH = pl.DeviceIdType.MESH
F32 = jnp.float32
BF16 = jnp.bfloat16
HD = 128
HL = 3
HW = HL * HD
SEQ = 1024
TOK = 128
COLS = 768
CH = 256
NCH = SEQ // CH
SCALE = HD ** (-0.5)
W_SCALE = SEQ ** (-0.5)
SEGMENTS = (
    ((0, 96, 0, 0), (96, 32, 1, 0)),
    ((0, 64, 1, 32), (64, 64, 0, 96)),
    ((0, 32, 0, 160), (32, 96, 1, 96)),
)
N_QKV = 21
WIDTH = (COLS, COLS // 2, COLS // 2)
PHASES = len(WIDTH)


def nt(a, b):
    return lax.dot_general(a, b, (((1,), (1,)), ((), ())), preferred_element_type=F32)


def nn(a, b):
    return lax.dot_general(a, b, (((1,), (0,)), ((), ())), preferred_element_type=F32)


def stats(source):
    wide = source.astype(F32)
    centred = wide - jnp.mean(wide, axis=-1, keepdims=True)
    inv = lax.rsqrt(jnp.mean(centred * centred, axis=-1, keepdims=True) + 1e-06)
    return centred * inv, inv


def norm_back(grad_n, source, gain):
    x_hat, inv = stats(source)
    u = grad_n * gain
    return inv * (
        u
        - jnp.mean(u, axis=-1, keepdims=True)
        - x_hat * jnp.mean(u * x_hat, axis=-1, keepdims=True)
    )


def kernel(
    q_in, k_in, v_in, ids_row, ids_col, qgain, kgain, w_in, gy,
    gq, gk, gv, gw,
    qkv, qn, kn, knt, vt, gyo, wb, prob, pg, rsr, att, ga, dk, dv,
    *stage,
):
    acc, cbuf, crecv, xrecv, zsend, zrecv, fsend, frecv = (
        stage[PHASES * i : PHASES * (i + 1)] for i in range(8)
    )
    (
        s_own, s_qkv, r_qkv, s_w, r_w, s_gy, r_gy, s_rs, r_rs, s_at, r_at,
        s_c, r_c, s_x, r_x, s_z, r_z, s_f, r_f, line_sem,
    ) = stage[PHASES * 8 :]
    f = lax.axis_index("fsdp")
    s = lax.axis_index("seq")
    zl, x, c = f // 8, (f // 2) % 4, f % 2
    y, zh = s // 2, s % 2
    oc = 1 - c
    ozh = 1 - zh
    xf = (x + 2) % 4
    xlo, xhi = x % 2, x // 2

    def dev(zl_=None, x_=None, c_=None, y_=None, zh_=None):
        zl_ = zl if zl_ is None else zl_
        x_ = x if x_ is None else x_
        c_ = c if c_ is None else c_
        y_ = y if y_ is None else y_
        zh_ = zh if zh_ is None else zh_
        return (zl_ * 8 + x_ * 2 + c_, y_ * 2 + zh_)

    def send(src, dst, ss, rs, where):
        return pltpu.make_async_remote_copy(
            src_ref=src, dst_ref=dst, send_sem=ss, recv_sem=rs,
            device_id=where, device_id_type=MESH,
        )

    offs = [(dy, 1) for dy in range(4)] + [(dy, 0) for dy in range(1, 4)]

    def seq_partner(dy, dz, sign=1):
        yy = (y + sign * dy + 4) % 4
        zz = (zh + dz) % 2
        return yy, zz

    barrier = pltpu.get_barrier_semaphore()
    partners = [dev(y_=a, zh_=b) for a, b in (seq_partner(dy, dz) for dy, dz in offs)]
    partners += [dev(x_=(x + o) % 4) for o in (1, 2, 3)]
    partners += [dev(zl_=(zl + o) % 4) for o in (1, 2, 3)]
    partners += [dev(c_=oc), dev(x_=xf, zh_=ozh)]
    for p in partners:
        pl.semaphore_signal(barrier, inc=1, device_id=p, device_id_type=MESH)
    pl.semaphore_wait(barrier, len(partners))

    same = xhi == zh
    w_own = wb.at[xhi, zl, xlo, c]
    w_swap = send(w_in, wb.at[1 - xhi, zl, xlo, c], s_w.at[0], r_w.at[0], dev(x_=xf, zh_=ozh))
    w_copy = pltpu.make_async_copy(w_in, w_own, s_own.at[3])

    sources = (q_in, k_in, v_in)
    qkv_copies = []
    for i, (dy, dz) in enumerate(offs):
        yy, zz = seq_partner(dy, dz)
        ps = yy * 2 + zz
        cols = pl.ds(pl.multiple_of(ps * HW, 128), HW)
        rows = pl.ds(pl.multiple_of(s * TOK, TOK), TOK)
        for a in range(3):
            n = i * 3 + a
            qkv_copies.append(
                send(sources[a].at[:, cols], qkv.at[a, rows, :], s_qkv.at[n], r_qkv.at[n],
                     dev(y_=yy, zh_=zz))
            )
    own_copies = []
    for a in range(3):
        cols = pl.ds(pl.multiple_of(s * HW, 128), HW)
        rows = pl.ds(pl.multiple_of(s * TOK, TOK), TOK)
        own_copies.append(
            pltpu.make_async_copy(sources[a].at[:, cols], qkv.at[a, rows, :], s_own.at[a])
        )
    def start_exchange():
        @pl.when(same)
        def _():
            w_copy.start()

        @pl.when(jnp.logical_not(same))
        def _():
            w_swap.start()

        for cp in qkv_copies[12:]:
            cp.start()
        for cp in own_copies:
            cp.start()

    def swapped():
        @pl.when(same)
        def _():
            w_copy.wait()

        @pl.when(jnp.logical_not(same))
        def _():
            w_swap.wait()

    wz = [
        send(w_own, w_own, s_w.at[o], r_w.at[o], dev(zl_=(zl + o) % 4)) for o in (1, 2, 3)
    ]
    w_line = wb.at[xhi, :, xlo, c]
    wx = [
        send(w_line, w_line, s_w.at[3 + o], r_w.at[3 + o], dev(x_=(x + o) % 4))
        for o in (1, 2, 3)
    ]
    wc = []
    for i in range(2):
        half = wb.at[i, :, :, c]
        wc.append(send(half, half, s_w.at[7 + i], r_w.at[7 + i], dev(c_=oc)))

    def weights_line():
        for cp in wz:
            cp.start()

    def heads_across():
        for cp in qkv_copies[:12]:
            cp.start()

    def weights_cross():
        for cp in wz:
            cp.wait()
        for cp in wx:
            cp.start()

    def weights_plane():
        for cp in wx:
            cp.wait()
        for cp in wc:
            cp.start()

    left, right = pl.ds(0, COLS // 2), pl.ds(COLS // 2, COLS // 2)
    gy_left = []
    for t in range(2):
        part = (pl.ds(t * (SEQ // 2), SEQ // 2), left)
        gy_left.append(
            send(gy.at[part], gyo.at[part], s_gy.at[NCH + t], r_gy.at[NCH + t], dev(zh_=ozh))
        )
    gy_right = []
    for t in range(NCH):
        part = (pl.ds(t * CH, CH), right)
        gy_right.append(send(gy.at[part], gyo.at[part], s_gy.at[t], r_gy.at[t], dev(zh_=ozh)))

    def sent_heads():
        for cp in own_copies:
            cp.wait()
        for cp in qkv_copies:
            cp.wait_send()

    gy_all = gy_left + gy_right

    def send_grad_y(*which):
        for n in which:
            gy_all[n].start()

    def sent_grad_y(*which):
        for n in which:
            gy_all[n].wait_send()

    def got_heads():
        for cp in qkv_copies:
            cp.wait_recv()

    gain_q = qgain[...]
    gain_k = kgain[...]
    def norms(h):
        hc = pl.ds(h * HD, HD)

        def norm_step(t, carry):
            rows = pl.ds(pl.multiple_of(t * CH, CH), CH)
            qh, _ = stats(qkv[0, rows, hc])
            qn[rows, hc] = (qh * gain_q).astype(BF16)
            kh, _ = stats(qkv[1, rows, hc])
            knv = kh * gain_k
            kn[rows, hc] = knv.astype(BF16)
            knt[hc, rows] = knv.T.astype(BF16)
            vt[hc, rows] = qkv[2, rows, hc].astype(F32).T.astype(BF16)
            return carry

        lax.fori_loop(0, NCH, norm_step, 0)

    def line_signal():
        for o in (1, 2, 3):
            pl.semaphore_signal(
                line_sem, inc=1, device_id=dev(zl_=(zl + o) % 4), device_id_type=MESH
            )

    def line_wait():
        pl.semaphore_wait(line_sem, 3)

    def att_copy(t, o):
        tile = att.at[
            :,
            pl.ds(pl.multiple_of(y * 192, 16), 192),
            pl.ds(pl.multiple_of(t * CH, CH), CH),
        ]
        n = t * 3 + o - 1
        return send(tile, tile, s_at.at[n], r_at.at[n], dev(y_=(y + o) % 4))

    def forward():
        def fwd_step(t, carry):
            rows = pl.ds(pl.multiple_of(t * CH, CH), CH)
            keep = ids_col[:, 0:1] == ids_row[:, rows]
            for h in range(HL):
                hc = pl.ds(h * HD, HD)
                st = nt(kn[:, hc], qn[rows, hc]) * SCALE
                st = jnp.where(keep, st, -1e30)
                top = jnp.max(st, axis=0, keepdims=True)
                e = jnp.exp(st - top)
                total = jnp.sum(e, axis=0, keepdims=True)
                pt = e * (1.0 / total)
                prob[h, :, rows] = pt
                at = nn(vt[hc, :], pt.astype(BF16)).astype(BF16)
                for first, count, half, place in SEGMENTS[h]:
                    at_rows = pl.ds(pl.multiple_of(y * 192 + place, 16), count)
                    att[half, at_rows, rows] = at[first : first + count, :]
            for o in (1, 2, 3):
                att_copy(t, o).start()
            return carry

        lax.fori_loop(0, NCH, fwd_step, 0)

    def got_weights():
        for cp in wc:
            cp.wait()

    def got_attended():
        def step(t, carry):
            for o in (1, 2, 3):
                att_copy(t, o).wait()
            return carry

        lax.fori_loop(0, NCH, step, 0)

    rs_copies = {}

    def grad_chunk(t):
        rows = pl.ds(t * CH, CH)
        if t == 0:
            for cp in gy_left:
                cp.wait_recv()
        gy_right[t].wait_recv()
        for o in (1, 2, 3, 0):
            yy = (y + o) % 4
            blk_own = wb[zh, yy].reshape(HW, COLS)
            blk_other = wb[ozh, yy].reshape(HW, COLS)
            val = nt(gy[rows, :], blk_own) + nt(gyo[rows, :], blk_other)
            pg[yy, rows, :] = val.astype(BF16)
            if o:
                cp = send(pg.at[yy, rows, :], rsr.at[o - 1, rows, :],
                          s_rs.at[t * 3 + o - 1], r_rs.at[t * 3 + o - 1], dev(y_=yy))
                rs_copies[(t, o)] = cp
                cp.start()

    def backward_chunk(t):
        rows = pl.ds(t * CH, CH)
        for o in (1, 2, 3):
            rs_copies[(t, o)].wait()
        total = pg[y, rows, :].astype(F32)
        for o in range(3):
            total = total + rsr[o, rows, :].astype(F32)
        ga[...] = total.astype(BF16)

        def head(h, carry):
            hc = pl.ds(pl.multiple_of(h * HD, HD), HD)
            do = ga[:, hc]
            dpt = nt(qkv[2, :, hc], do)
            pt = prob[h, :, rows]
            delta = jnp.sum(pt * dpt, axis=0, keepdims=True)
            dst = (pt * (dpt - delta) * SCALE).astype(BF16)
            dv_new = nn(pt.astype(BF16), do)
            dk_new = nn(dst, qn[rows, hc])
            if t == 0:
                dv[:, hc] = dv_new
                dk[:, hc] = dk_new
            else:
                dv[:, hc] += dv_new
                dk[:, hc] += dk_new
            dqt = nn(knt[hc, :], dst)
            gq[h, rows, :] = norm_back(dqt.T, qkv[0, rows, hc], gain_q).astype(BF16)
            return carry

        lax.fori_loop(0, HL, head, 0)

    core_copies = [
        send(cbuf[p], crecv[p], s_c.at[p], r_c.at[p], dev(c_=oc)) for p in range(PHASES)
    ]

    def weight_products(p):
        wide = COLS // 2
        source, first = ((gy, 0), (gyo, 0), (gyo, wide))[p]
        for half, mine in ((oc, False), (c, True)):
            for n in range(WIDTH[p] // wide):
                val = nn(att[half], source[:, pl.ds(first + n * wide, wide)])
                val = val.reshape(4, 4, 48, wide)
                to = pl.ds(n * wide, wide)
                if mine:
                    acc[p][:, :, :, to] = val
                else:
                    cbuf[p][:, :, :, to] = val.astype(BF16)
            if not mine:
                core_copies[p].start()

    x_copies = {}

    def to_x(p):
        core_copies[p].wait()

        def step(i, carry):
            val = acc[p][i] + crecv[p][i].astype(F32)
            acc[p][i] = val
            cbuf[p][i] = val.astype(BF16)
            return carry

        lax.fori_loop(0, 4, step, 0)
        for o in (1, 2, 3):
            xx = (x + o) % 4
            quarter = (xx % 2) * 2 + xx // 2
            n = p * 3 + o - 1
            cp = send(cbuf[p].at[:, quarter], xrecv[p].at[o - 1], s_x.at[n], r_x.at[n],
                      dev(x_=xx))
            x_copies[(p, o)] = cp
            cp.start()

    z_copies = {}

    def to_z(p):
        for o in (1, 2, 3):
            x_copies[(p, o)].wait()
        quarter = xlo * 2 + xhi

        def step(i, carry):
            val = acc[p][i, quarter]
            for o in range(3):
                val = val + xrecv[p][o, i].astype(F32)
            acc[p][i, quarter] = val
            zsend[p][i] = val.astype(BF16)
            return carry

        lax.fori_loop(0, 4, step, 0)
        for o in (1, 2, 3):
            zz = (zl + o) % 4
            n = p * 3 + o - 1
            cp = send(zsend[p].at[zz], zrecv[p].at[o - 1], s_z.at[n], r_z.at[n], dev(zl_=zz))
            z_copies[(p, o)] = cp
            cp.start()

    def reduced(p):
        for o in (1, 2, 3):
            z_copies[(p, o)].wait()
        val = acc[p][zl, xlo * 2 + xhi]
        for o in range(3):
            val = val + zrecv[p][o].astype(F32)
        return val * W_SCALE

    mine_rows = pl.ds(pl.multiple_of(xhi * 48, 16), 48)
    other_rows = pl.ds(pl.multiple_of((1 - xhi) * 48, 16), 48)
    f_x = send(fsend[0], frecv[0].at[0], s_f.at[0], r_f.at[0], dev(x_=xf))
    f_z = [
        send(fsend[p], frecv[p].at[0], s_f.at[p], r_f.at[p], dev(zh_=ozh))
        for p in range(1, PHASES)
    ]
    f_xz = [
        send(fsend[p], frecv[p].at[1], s_f.at[2 + p], r_f.at[2 + p], dev(x_=xf, zh_=ozh))
        for p in range(1, PHASES)
    ]

    def finish(p):
        val = reduced(p)
        if p == 0:

            @pl.when(same)
            def _():
                gw[mine_rows, :] = val

            @pl.when(jnp.logical_not(same))
            def _():
                fsend[0][...] = val.astype(BF16)
                f_x.start()

        else:
            fsend[p][...] = val.astype(BF16)

            @pl.when(same)
            def _():
                f_z[p - 1].start()

            @pl.when(jnp.logical_not(same))
            def _():
                f_xz[p - 1].start()

    def collect():
        @pl.when(same)
        def _():
            f_x.wait_recv()
            gw[other_rows, :] = frecv[0][0].astype(F32)
            for cp in f_z:
                cp.wait_send()

        @pl.when(jnp.logical_not(same))
        def _():
            f_x.wait_send()
            for p in range(1, PHASES):
                to = pl.ds((p - 1) * (COLS // 2), COLS // 2)
                f_z[p - 1].wait_recv()
                gw[mine_rows, to] = frecv[p][0].astype(F32)
                f_xz[p - 1].wait()
                gw[other_rows, to] = frecv[p][1].astype(F32)

    def key_grads():
        for h in range(HL):
            hc = pl.ds(h * HD, HD)

            def key_step(t, carry, h=h, hc=hc):
                rows = pl.ds(pl.multiple_of(t * CH, CH), CH)
                gk[h, rows, :] = norm_back(dk[rows, hc], qkv[1, rows, hc], gain_k).astype(BF16)
                gv[h, rows, :] = dv[rows, hc].astype(BF16)
                return carry

            lax.fori_loop(0, NCH, key_step, 0)

    start_exchange()
    swapped()
    weights_line()
    heads_across()
    sent_heads()
    got_heads()
    weights_cross()
    line_signal()
    norms(0)
    line_wait()
    send_grad_y(0, 1, 2, 3, 4, 5)
    norms(1)
    norms(2)
    forward()
    weights_plane()
    got_weights()
    grad_chunk(0)
    grad_chunk(1)
    got_attended()
    weight_products(0)
    weight_products(1)
    grad_chunk(2)
    backward_chunk(0)
    to_x(0)
    to_x(1)
    grad_chunk(3)
    weight_products(2)
    backward_chunk(1)
    to_x(2)
    to_z(0)
    backward_chunk(2)
    to_z(1)
    backward_chunk(3)
    finish(0)
    to_z(2)
    finish(1)
    key_grads()
    finish(2)
    sent_grad_y(0, 1, 2, 3, 4, 5)
    collect()


def local(queries, keys, values, image_ids, q_gain, k_gain, w_out, grad_y):
    ids_col = jnp.broadcast_to(image_ids.reshape(SEQ, 1), (SEQ, 128))
    vm = pl.BlockSpec(memory_space=pltpu.VMEM)
    hb = pl.BlockSpec(memory_space=pl.ANY)
    dma = lambda n: pltpu.SemaphoreType.DMA((n,))
    vmem = pltpu.VMEM
    scratch = [
        vmem((3, SEQ, HW), BF16),
        vmem((SEQ, HW), BF16),
        vmem((SEQ, HW), BF16),
        vmem((HW, SEQ), BF16),
        vmem((HW, SEQ), BF16),
        vmem((SEQ, COLS), BF16),
        vmem((2, 4, 2, 2, 96, COLS), BF16),
        vmem((HL, SEQ, SEQ), F32),
        vmem((4, SEQ, HW), BF16),
        vmem((3, SEQ, HW), BF16),
        vmem((2, 768, SEQ), BF16),
        vmem((CH, HW), BF16),
        vmem((SEQ, HW), F32),
        vmem((SEQ, HW), F32),
        *[vmem((4, 4, 48, w), F32) for w in WIDTH],
        *[vmem((4, 4, 48, w), BF16) for w in WIDTH],
        *[vmem((4, 4, 48, w), BF16) for w in WIDTH],
        *[vmem((3, 4, 48, w), BF16) for w in WIDTH],
        *[vmem((4, 48, w), BF16) for w in WIDTH],
        *[vmem((3, 48, w), BF16) for w in WIDTH],
        *[vmem((48, w), BF16) for w in WIDTH],
        *[vmem((2, 48, w), BF16) for w in WIDTH],
        dma(4),
        dma(N_QKV), dma(N_QKV),
        dma(9), dma(9),
        dma(NCH + 2), dma(NCH + 2),
        dma(3 * NCH), dma(3 * NCH),
        dma(3 * NCH), dma(3 * NCH),
        dma(PHASES), dma(PHASES),
        dma(3 * PHASES), dma(3 * PHASES),
        dma(3 * PHASES), dma(3 * PHASES),
        dma(5), dma(5),
        pltpu.SemaphoreType.REGULAR,
    ]
    gq, gk, gv, gw = pl.pallas_call(
        kernel,
        out_shape=(
            jax.ShapeDtypeStruct((HL, SEQ, HD), BF16),
            jax.ShapeDtypeStruct((HL, SEQ, HD), BF16),
            jax.ShapeDtypeStruct((HL, SEQ, HD), BF16),
            jax.ShapeDtypeStruct((96, COLS), F32),
        ),
        in_specs=[hb, hb, hb, vm, vm, vm, vm, vm, vm],
        out_specs=(vm, vm, vm, vm),
        scratch_shapes=scratch,
        compiler_params=pltpu.CompilerParams(
            collective_id=0, has_side_effects=True, vmem_limit_bytes=62 * 1024 * 1024
        ),
        name="attention_backward",
    )(
        queries, keys, values, image_ids, ids_col,
        q_gain.reshape(1, HD), k_gain.reshape(1, HD), w_out, grad_y,
    )
    heads = lambda a: a.transpose(1, 0, 2)
    return heads(gq), heads(gk), heads(gv), gw


def solution(mesh):
    in_specs = (
        P(("fsdp", "seq"), None),
        P(("fsdp", "seq"), None),
        P(("fsdp", "seq"), None),
        P("fsdp", None),
        P(),
        P(),
        P("fsdp", "seq"),
        P("fsdp", "seq"),
    )
    out_specs = (
        P("fsdp", "seq", None),
        P("fsdp", "seq", None),
        P("fsdp", "seq", None),
        P("fsdp", "seq"),
    )
    return jax.shard_map(local, mesh=mesh, in_specs=in_specs, out_specs=out_specs, check_vma=False)
```

time: 246 us -> 210 us (0.85); the launches traced: 246 us -> 206 us
  Pallas kernels: 238 us -> 199 us
    pallas_call x1, Pallas kernels: 238 us -> 199 us  [local(): pl.pallas_call(kernel, out_shape=(jax.ShapeDtypeStruct((HL, SEQ, HD), BF1...]
where the time goes in v2:
time: 210 us; the launch traced here: 206 us
  Pallas kernels  199 us (95%)
  local copies, waits for them, and re-layouts  6.35 us (3%)
    pallas_call x1, Pallas kernels, local(): pl.pallas_call(kernel, out_shape=(jax.ShapeDtypeStruct((HL, SEQ, HD), BF1...  199 us
    unnamed x10, local copies, waits for them, and re-layouts  4.66 us

profile of v2, /device:TPU:36, one launch (start us, length us, event | category | flops | bytes accessed | tf_op | source)
XLA Modules:
  0.0 206.0 jit_solution(3465861389235408035)
XLA Ops:
  0.6 1.7 broadcast_in_dim.8.ids_col
  2.3 199.0 %attention_backward.1 = (bf16[3,1024,128]{2,1,0:T(8,128)(2,1)}, bf16[3,1024,128]{2,1,0:T(8,128)(2,1)}, bf16[3,1024,128]{2,1,0:T(8,128)(2,1)}, f32[96,768]{1,0:T(8,128)}) custom-call(bf16[128,3072]{1,0:T(8,128)(2,1)} %q_in.1, bf16[128,3072]{1,0:T(8,128)(2,1)} %k_in.1, bf16[128,3072]{1,0:T(8,128)(2,1)} %v_in.1, s32[1,1024]{1,0:T(1,128)} %ids_row.1, ...), custom_call_target="tpu_custom_call" | custom-call | tf_op jit(solution)/shard_map/attention_backward/pallas_call | solution.py:562
  201.3 0.0 copy-start.1
  201.3 0.0 copy-start
  201.3 2.2 %copy.16 = bf16[1024,3,128]{2,0,1:T(8,128)(2,1)} copy(bf16[1024,3,128]{2,0,1:T(8,128)(2,1)} %bitcast.8) | data formatting | bytes 1572864
  203.5 0.0 copy-done.1
  203.5 0.0 copy-start.2
  203.5 0.9 copy.17
  204.4 0.0 copy-done
  204.4 0.9 copy.18
  205.3 0.0 copy-done.2
  205.3 0.7 copy.19
Async XLA Ops:
  201.3 2.2 %copy-start.1 = (bf16[3,1024,128]{2,1,0:T(8,128)(2,1)S(1)}, bf16[3,1024,128]{2,1,0:T(8,128)(2,1)}, u32[]{:S(2)}) copy-start(bf16[3,1024,128]{2,1,0:T(8,128)(2,1)} %get-tuple-element.9) | copy-start | bytes 2359300
  201.3 3.1 %copy-start = (bf16[3,1024,128]{2,1,0:T(8,128)(2,1)S(1)}, bf16[3,1024,128]{2,1,0:T(8,128)(2,1)}, u32[]{:S(2)}) copy-start(bf16[3,1024,128]{2,1,0:T(8,128)(2,1)} %get-tuple-element.10) | copy-start | bytes 2359300
  203.5 1.8 copy-start.2

commit v3 on v2

--- a/solution.py
+++ b/solution.py
@@ -54,7 +54,7 @@
 
 
 def kernel(
-    q_in, k_in, v_in, ids_row, ids_col, qgain, kgain, w_in, gy,
+    q_in, k_in, v_in, ids_row, qgain, kgain, w_in, gy,
     gq, gk, gv, gw,
     qkv, qn, kn, knt, vt, gyo, wb, prob, pg, rsr, att, ga, dk, dv,
     *stage,
@@ -64,7 +64,7 @@
     )
     (
         s_own, s_qkv, r_qkv, s_w, r_w, s_gy, r_gy, s_rs, r_rs, s_at, r_at,
-        s_c, r_c, s_x, r_x, s_z, r_z, s_f, r_f, line_sem,
+        s_c, r_c, s_x, r_x, s_z, r_z, s_f, r_f, line_sem, ids_col,
     ) = stage[PHASES * 8 :]
     f = lax.axis_index("fsdp")
     s = lax.axis_index("seq")
@@ -156,33 +156,39 @@
     wz = [
         send(w_own, w_own, s_w.at[o], r_w.at[o], dev(zl_=(zl + o) % 4)) for o in (1, 2, 3)
     ]
-    w_line = wb.at[xhi, :, xlo, c]
-    wx = [
-        send(w_line, w_line, s_w.at[3 + o], r_w.at[3 + o], dev(x_=(x + o) % 4))
-        for o in (1, 2, 3)
-    ]
+    wx = []
+    for j in range(4):
+        shard = wb.at[xhi, (zl - j + 4) % 4, xlo, c]
+        wx.append([
+            send(shard, shard, s_w.at[6 + j * 3 + o - 1], r_w.at[6 + j * 3 + o - 1],
+                 dev(x_=(x + o) % 4))
+            for o in (1, 2, 3)
+        ])
     wc = []
     for i in range(2):
         half = wb.at[i, :, :, c]
-        wc.append(send(half, half, s_w.at[7 + i], r_w.at[7 + i], dev(c_=oc)))
+        wc.append(send(half, half, s_w.at[4 + i], r_w.at[4 + i], dev(c_=oc)))
 
     def weights_line():
         for cp in wz:
             cp.start()
+        for cp in wx[0]:
+            cp.start()
 
     def heads_across():
         for cp in qkv_copies[:12]:
             cp.start()
 
     def weights_cross():
-        for cp in wz:
-            cp.wait()
-        for cp in wx:
-            cp.start()
+        for j in range(1, 4):
+            wz[j - 1].wait()
+            for cp in wx[j]:
+                cp.start()
 
     def weights_plane():
-        for cp in wx:
-            cp.wait()
+        for group in wx:
+            for cp in group:
+                cp.wait()
         for cp in wc:
             cp.start()
 
@@ -220,6 +226,12 @@
 
     gain_q = qgain[...]
     gain_k = kgain[...]
+    def image_columns():
+        for t in range(SEQ // HD):
+            part = pl.ds(t * HD, HD)
+            ids = jnp.broadcast_to(ids_row[:, part].astype(F32), (HD, HD))
+            ids_col[part, :] = ids.T
+
     def norms(h):
         hc = pl.ds(h * HD, HD)
 
@@ -254,10 +266,10 @@
         n = t * 3 + o - 1
         return send(tile, tile, s_at.at[n], r_at.at[n], dev(y_=(y + o) % 4))
 
-    def forward():
+    def forward(first, last):
         def fwd_step(t, carry):
             rows = pl.ds(pl.multiple_of(t * CH, CH), CH)
-            keep = ids_col[:, 0:1] == ids_row[:, rows]
+            keep = ids_col[:, 0:1] == ids_row[:, rows].astype(F32)
             for h in range(HL):
                 hc = pl.ds(h * HD, HD)
                 st = nt(kn[:, hc], qn[rows, hc]) * SCALE
@@ -275,7 +287,7 @@
                 att_copy(t, o).start()
             return carry
 
-        lax.fori_loop(0, NCH, fwd_step, 0)
+        lax.fori_loop(first, last, fwd_step, 0)
 
     def got_weights():
         for cp in wc:
@@ -291,12 +303,15 @@
 
     rs_copies = {}
 
+    def got_left():
+        for cp in gy_left:
+            cp.wait_recv()
+
+    def got_right(t):
+        gy_right[t].wait_recv()
+
     def grad_chunk(t):
         rows = pl.ds(t * CH, CH)
-        if t == 0:
-            for cp in gy_left:
-                cp.wait_recv()
-        gy_right[t].wait_recv()
         for o in (1, 2, 3, 0):
             yy = (y + o) % 4
             blk_own = wb[zh, yy].reshape(HW, COLS)
@@ -477,39 +492,47 @@
             lax.fori_loop(0, NCH, key_step, 0)
 
     start_exchange()
+    heads_across()
+    image_columns()
+    sent_heads()
+    send_grad_y(0)
+    got_heads()
     swapped()
     weights_line()
-    heads_across()
-    sent_heads()
-    got_heads()
+    norms(0)
+    norms(1)
+    norms(2)
+    forward(0, 3)
     weights_cross()
     line_signal()
-    norms(0)
     line_wait()
-    send_grad_y(0, 1, 2, 3, 4, 5)
-    norms(1)
-    norms(2)
-    forward()
+    send_grad_y(1, 2, 3, 4, 5)
+    forward(3, 4)
     weights_plane()
-    got_weights()
-    grad_chunk(0)
-    grad_chunk(1)
     got_attended()
     weight_products(0)
+    got_weights()
+    got_left()
     weight_products(1)
-    grad_chunk(2)
-    backward_chunk(0)
     to_x(0)
     to_x(1)
+    got_right(0)
+    grad_chunk(0)
+    got_right(1)
+    grad_chunk(1)
+    backward_chunk(0)
+    got_right(2)
+    grad_chunk(2)
+    to_z(0)
+    backward_chunk(1)
+    got_right(3)
+    weight_products(2)
     grad_chunk(3)
-    weight_products(2)
-    backward_chunk(1)
     to_x(2)
-    to_z(0)
     backward_chunk(2)
     to_z(1)
+    finish(0)
     backward_chunk(3)
-    finish(0)
     to_z(2)
     finish(1)
     key_grads()
@@ -519,7 +542,6 @@
 
 
 def local(queries, keys, values, image_ids, q_gain, k_gain, w_out, grad_y):
-    ids_col = jnp.broadcast_to(image_ids.reshape(SEQ, 1), (SEQ, 128))
     vm = pl.BlockSpec(memory_space=pltpu.VMEM)
     hb = pl.BlockSpec(memory_space=pl.ANY)
     dma = lambda n: pltpu.SemaphoreType.DMA((n,))
@@ -549,7 +571,7 @@
         *[vmem((2, 48, w), BF16) for w in WIDTH],
         dma(4),
         dma(N_QKV), dma(N_QKV),
-        dma(9), dma(9),
+        dma(18), dma(18),
         dma(NCH + 2), dma(NCH + 2),
         dma(3 * NCH), dma(3 * NCH),
         dma(3 * NCH), dma(3 * NCH),
@@ -558,6 +580,7 @@
         dma(3 * PHASES), dma(3 * PHASES),
         dma(5), dma(5),
         pltpu.SemaphoreType.REGULAR,
+        vmem((SEQ, HD), F32),
     ]
     gq, gk, gv, gw = pl.pallas_call(
         kernel,
@@ -567,7 +590,7 @@
             jax.ShapeDtypeStruct((HL, SEQ, HD), BF16),
             jax.ShapeDtypeStruct((96, COLS), F32),
         ),
-        in_specs=[hb, hb, hb, vm, vm, vm, vm, vm, vm],
+        in_specs=[hb, hb, hb, vm, vm, vm, vm, vm],
         out_specs=(vm, vm, vm, vm),
         scratch_shapes=scratch,
         compiler_params=pltpu.CompilerParams(
@@ -575,7 +598,7 @@
         ),
         name="attention_backward",
     )(
-        queries, keys, values, image_ids, ids_col,
+        queries, keys, values, image_ids,
         q_gain.reshape(1, HD), k_gain.reshape(1, HD), w_out, grad_y,
     )
     heads = lambda a: a.transpose(1, 0, 2)

time: 210 us -> 200 us (0.952); the launches traced: 206 us -> 199 us
  Pallas kernels: 199 us -> 194 us
    pallas_call x1, Pallas kernels: 199 us -> 194 us  [local(): pl.pallas_call(kernel, out_shape=(jax.ShapeDtypeStruct((HL, SEQ, HD), BF1...]
where the time goes in v3:
time: 200 us; the launch traced here: 199 us
  Pallas kernels  194 us (97%)
  local copies, waits for them, and re-layouts  4.66 us (2%)
    pallas_call x1, Pallas kernels, local(): pl.pallas_call(kernel, out_shape=(jax.ShapeDtypeStruct((HL, SEQ, HD), BF1...  194 us
    unnamed x10, local copies, waits for them, and re-layouts  4.66 us

profile of v3, /device:TPU:36, one launch (start us, length us, event | category | flops | bytes accessed | tf_op | source)
XLA Modules:
  0.0 199.3 jit_solution(3021375392717629416)
XLA Ops:
  0.6 194.0 %attention_backward.1 = (bf16[3,1024,128]{2,1,0:T(8,128)(2,1)}, bf16[3,1024,128]{2,1,0:T(8,128)(2,1)}, bf16[3,1024,128]{2,1,0:T(8,128)(2,1)}, f32[96,768]{1,0:T(8,128)}) custom-call(bf16[128,3072]{1,0:T(8,128)(2,1)} %q_in.1, bf16[128,3072]{1,0:T(8,128)(2,1)} %k_in.1, bf16[128,3072]{1,0:T(8,128)(2,1)} %v_in.1, s32[1,1024]{1,0:T(1,128)} %ids_row.1, ...), custom_call_target="tpu_custom_call" | custom-call | tf_op jit(solution)/shard_map/attention_backward/pallas_call | solution.py:585
  194.6 0.0 copy-start.1
  194.6 0.0 copy-start
  194.6 2.2 %copy.16 = bf16[1024,3,128]{2,0,1:T(8,128)(2,1)} copy(bf16[1024,3,128]{2,0,1:T(8,128)(2,1)} %bitcast.7) | data formatting | bytes 1572864
  196.8 0.0 copy-done.1
  196.8 0.0 copy-start.2
  196.8 0.9 copy.17
  197.7 0.0 copy-done
  197.7 0.9 copy.18
  198.6 0.0 copy-done.2
  198.6 0.7 copy.19
Async XLA Ops:
  194.6 2.2 %copy-start.1 = (bf16[3,1024,128]{2,1,0:T(8,128)(2,1)S(1)}, bf16[3,1024,128]{2,1,0:T(8,128)(2,1)}, u32[]{:S(2)}) copy-start(bf16[3,1024,128]{2,1,0:T(8,128)(2,1)} %get-tuple-element.9) | copy-start | bytes 2359300
  194.6 3.1 %copy-start = (bf16[3,1024,128]{2,1,0:T(8,128)(2,1)S(1)}, bf16[3,1024,128]{2,1,0:T(8,128)(2,1)}, u32[]{:S(2)}) copy-start(bf16[3,1024,128]{2,1,0:T(8,128)(2,1)} %get-tuple-element.10) | copy-start | bytes 2359300
  196.8 1.8 copy-start.2

commit v4 on v3

--- a/solution.py
+++ b/solution.py
@@ -494,20 +494,20 @@
     start_exchange()
     heads_across()
     image_columns()
+    swapped()
+    weights_line()
     sent_heads()
     send_grad_y(0)
     got_heads()
-    swapped()
-    weights_line()
     norms(0)
     norms(1)
     norms(2)
-    forward(0, 3)
+    forward(0, 2)
     weights_cross()
     line_signal()
     line_wait()
     send_grad_y(1, 2, 3, 4, 5)
-    forward(3, 4)
+    forward(2, 4)
     weights_plane()
     got_attended()
     weight_products(0)
@@ -532,11 +532,11 @@
     backward_chunk(2)
     to_z(1)
     finish(0)
+    to_z(2)
     backward_chunk(3)
-    to_z(2)
     finish(1)
+    finish(2)
     key_grads()
-    finish(2)
     sent_grad_y(0, 1, 2, 3, 4, 5)
     collect()
 

time: 200 us -> 193 us (0.965)
  Pallas kernels: 194 us -> 186 us
    pallas_call x1, Pallas kernels: 194 us -> 186 us  [local(): pl.pallas_call(kernel, out_shape=(jax.ShapeDtypeStruct((HL, SEQ, HD), BF1...]
where the time goes in v4:
time: 193 us; the launch traced here: 192 us
  Pallas kernels  186 us (96%)
  local copies, waits for them, and re-layouts  4.66 us (2%)
    pallas_call x1, Pallas kernels, local(): pl.pallas_call(kernel, out_shape=(jax.ShapeDtypeStruct((HL, SEQ, HD), BF1...  186 us
    unnamed x10, local copies, waits for them, and re-layouts  4.66 us

profile of v4, /device:TPU:36, one launch (start us, length us, event | category | flops | bytes accessed | tf_op | source)
XLA Modules:
  0.0 191.6 jit_solution(11822853953616056945)
XLA Ops:
  0.6 186.3 %attention_backward.1 = (bf16[3,1024,128]{2,1,0:T(8,128)(2,1)}, bf16[3,1024,128]{2,1,0:T(8,128)(2,1)}, bf16[3,1024,128]{2,1,0:T(8,128)(2,1)}, f32[96,768]{1,0:T(8,128)}) custom-call(bf16[128,3072]{1,0:T(8,128)(2,1)} %q_in.1, bf16[128,3072]{1,0:T(8,128)(2,1)} %k_in.1, bf16[128,3072]{1,0:T(8,128)(2,1)} %v_in.1, s32[1,1024]{1,0:T(1,128)} %ids_row.1, ...), custom_call_target="tpu_custom_call" | custom-call | tf_op jit(solution)/shard_map/attention_backward/pallas_call | solution.py:585
  187.0 0.0 copy-start.1
  187.0 0.0 copy-start
  187.0 2.2 %copy.16 = bf16[1024,3,128]{2,0,1:T(8,128)(2,1)} copy(bf16[1024,3,128]{2,0,1:T(8,128)(2,1)} %bitcast.7) | data formatting | bytes 1572864
  189.2 0.0 copy-done.1
  189.2 0.0 copy-start.2
  189.2 0.9 copy.17
  190.0 0.0 copy-done
  190.0 0.9 copy.18
  190.9 0.0 copy-done.2
  190.9 0.7 copy.19
Async XLA Ops:
  187.0 2.2 %copy-start.1 = (bf16[3,1024,128]{2,1,0:T(8,128)(2,1)S(1)}, bf16[3,1024,128]{2,1,0:T(8,128)(2,1)}, u32[]{:S(2)}) copy-start(bf16[3,1024,128]{2,1,0:T(8,128)(2,1)} %get-tuple-element.9) | copy-start | bytes 2359300
  187.0 3.1 %copy-start = (bf16[3,1024,128]{2,1,0:T(8,128)(2,1)S(1)}, bf16[3,1024,128]{2,1,0:T(8,128)(2,1)}, u32[]{:S(2)}) copy-start(bf16[3,1024,128]{2,1,0:T(8,128)(2,1)} %get-tuple-element.10) | copy-start | bytes 2359300
  189.2 1.8 copy-start.2
